TPU v7x, 32 devices: a whole 2x2x4 slice. The times are simulated.
32 devices in a mesh: dp: 8 (over z, y), tensor: 4 (over x, core).
Axes of the slice: x: 2, y: 2, z: 4, core: 2. Of those that a mesh axis runs over, the one named last changes fastest.
Arguments:
- tokens: bfloat16 [65536, 512], P(('dp', 'tensor')), may hold values from -6 to 6
- segment_ids: int32 [128, 512], P('dp'), may hold values from 0 to 15, never falling along the last dimension, each value on 1 to 128 neighbouring positions
- row_lengths: int32 [128], P('dp'), may hold values from 256 to 512, as said below
- qkv_weight: bfloat16 [3, 512, 512], P(None, None, 'tensor'), may hold values from -6 to 6
- qv_bias: bfloat16 [2, 512], P(None, 'tensor'), may hold values from -3 to 3
- proj_weight: bfloat16 [512, 512], P('tensor'), may hold values from -6 to 6
- proj_bias: bfloat16 [512], replicated, may hold values from -3 to 3
- first_gain: bfloat16 [512], replicated, may hold values from 0.5 to 1.5
- first_shift: bfloat16 [512], replicated, may hold values from -3 to 3
- up_weight: bfloat16 [512, 2048], P(None, 'tensor'), may hold values from -6 to 6
- up_bias: bfloat16 [2048], P('tensor'), may hold values from -3 to 3
- down_weight: bfloat16 [2048, 512], P('tensor'), may hold values from -6 to 6
- down_bias: bfloat16 [512], replicated, may hold values from -3 to 3
- second_gain: bfloat16 [512], replicated, may hold values from 0.5 to 1.5
- second_shift: bfloat16 [512], replicated, may hold values from -3 to 3
- out_grad: bfloat16 [65536, 512], P(('dp', 'tensor')), may hold values from -6 to 6
Outputs:
- layer_out: bfloat16 [65536, 512], P(('dp', 'tensor'))
- tokens_grad: float32 [65536, 512], P(('dp', 'tensor'))
- qkv_weight_grad: float32 [3, 512, 512], P(None, None, 'tensor')
- qv_bias_grad: float32 [2, 512], P(None, 'tensor')
- proj_weight_grad: float32 [512, 512], P('tensor')
- proj_bias_grad: float32 [512], replicated
- first_gain_grad: float32 [512], replicated
- first_shift_grad: float32 [512], replicated
- up_weight_grad: float32 [512, 2048], P(None, 'tensor')
- up_bias_grad: float32 [2048], P('tensor')
- down_weight_grad: float32 [2048, 512], P('tensor')
- down_bias_grad: float32 [512], replicated
- second_gain_grad: float32 [512], replicated
- second_shift_grad: float32 [512], replicated
Inputs may be any that keep to these rules, and one draw needn't show every extreme that they name: `segment_ids`: ids never fall along a packed row; every id of 0 to 15 is used by 1 to 128 consecutive tokens of each row, one example of every row holding exactly 128. `row_lengths`: of the rows of one index of dp, one of the first two holds 512 tokens and the other 256; places at or past a row's length are padding.
All inputs are finite; a program needn't handle non-finite values.
Results may differ from a plain program's by a relative error of at most 0.022.
Values may be sent and summed in bfloat16 or wider, within the bound.
A program may use at most 256 MiB of HBM per device.

v0:
```python
import jax
import jax.numpy as jnp
from jax import lax
from jax.sharding import PartitionSpec as P

HEAD_DIM = 64
levels = 127.0
norm_eps = 1e-12
masked_score = -1e30


def quantize(values, peak_value):
    step_size = peak_value / levels
    scaled = values / step_size
    return (jnp.sign(scaled) * jnp.floor(jnp.abs(scaled) + 0.5), step_size)


def passes(values):
    return jnp.sign(values) * jnp.sign(values)


def exact_gelu(values):
    return jax.nn.gelu(values, approximate=False)


def group_rows(values):
    return lax.all_gather(values, "tensor", axis=0, tiled=True)


def reduce_rows(term_fn, own_rows):
    return lax.psum_scatter(
        term_fn(jnp.int32(0), lax.axis_size("tensor") * own_rows).astype(jnp.bfloat16),
        "tensor",
        scatter_dimension=0,
        tiled=True,
    ).astype(jnp.float32)


def norm_forward(values, gain_vec, shift_vec):
    centred = values - jnp.mean(values, axis=-1, keepdims=True)
    inverse = lax.rsqrt(jnp.mean(centred * centred, axis=-1, keepdims=True) + norm_eps)
    standard = centred * inverse
    return (standard * gain_vec + shift_vec, standard, inverse)


def norm_backward(incoming, standard, inverse, gain_vec):
    scaled = incoming * gain_vec
    centred = (
        scaled
        - jnp.mean(scaled, axis=-1, keepdims=True)
        - standard * jnp.mean(scaled * standard, axis=-1, keepdims=True)
    )
    return (centred * inverse, jnp.sum(incoming * standard, axis=0), jnp.sum(incoming, axis=0))


def allowed_mask(segments, lengths, seq_len):
    places = jnp.arange(seq_len)
    same_doc = segments[:, :, None] == segments[:, None, :]
    inside = places[None, None, :] < lengths[:, None, None]
    diagonal = places[:, None] == places[None, :]
    return same_doc & inside | diagonal[None]


def pair_scores(queries, keys_low, segments, lengths):
    scale_factor = queries.shape[-1] ** (-0.5)
    scores = (
        jnp.einsum("rqhe,rkhe->rhqk", queries, keys_low, preferred_element_type=jnp.float32)
        * scale_factor
    )
    allowed = allowed_mask(segments, lengths, queries.shape[1])
    return (jnp.where(allowed[:, None], scores, masked_score), scale_factor)


def attend_pair(pieces):
    queries, keys_low, values_low, segments, lengths = pieces
    scores, scale_factor = pair_scores(queries, keys_low, segments, lengths)
    top_score = jnp.max(scores, axis=-1, keepdims=True)
    weights = jnp.exp(scores - top_score)
    totals = jnp.sum(weights, axis=-1, keepdims=True)
    attn_probs = (weights / totals).astype(jnp.bfloat16)
    context = jnp.einsum(
        "rhqk,rkhe->rqhe", attn_probs, values_low, preferred_element_type=jnp.float32
    )
    return (context, top_score + jnp.log(totals))


def attend_back(pieces):
    queries, keys_low, values_low, segments, lengths, log_total, grad_context = pieces
    scores, scale_factor = pair_scores(queries, keys_low, segments, lengths)
    attn_probs = jnp.exp(scores - log_total)
    grad_values = jnp.einsum(
        "rhqk,rqhe->rkhe",
        attn_probs.astype(jnp.bfloat16),
        grad_context,
        preferred_element_type=jnp.float32,
    )
    grad_probs = jnp.einsum(
        "rqhe,rkhe->rhqk", grad_context, values_low, preferred_element_type=jnp.float32
    )
    centre = jnp.sum(grad_probs * attn_probs, axis=-1, keepdims=True)
    grad_scores = (attn_probs * (grad_probs - centre) * scale_factor).astype(jnp.bfloat16)
    grad_queries = jnp.einsum(
        "rhqk,rkhe->rqhe", grad_scores, keys_low, preferred_element_type=jnp.float32
    )
    grad_keys = jnp.einsum(
        "rhqk,rqhe->rkhe", grad_scores, queries, preferred_element_type=jnp.float32
    )
    return (grad_queries, grad_keys, grad_values)


def local(
    tokens,
    segment_ids,
    row_lengths,
    qkv_weight,
    qv_bias,
    proj_weight,
    proj_bias,
    first_gain,
    first_shift,
    up_weight,
    up_bias,
    down_weight,
    down_bias,
    second_gain,
    second_shift,
    out_grad,
):
    own_rows = tokens.shape[0]
    rows_here = segment_ids.shape[0]
    seq_len = segment_ids.shape[1]
    heads_here = qkv_weight.shape[2] // HEAD_DIM
    token_vals = tokens.astype(jnp.float32)
    qkv_vals = qkv_weight.astype(jnp.float32)
    proj_vals = proj_weight.astype(jnp.float32)
    up_vals = up_weight.astype(jnp.float32)
    down_vals = down_weight.astype(jnp.float32)
    top_qkv = jnp.max(jnp.abs(qkv_vals), axis=(1, 2))
    top_proj = jnp.max(jnp.abs(proj_vals))
    top_up = jnp.max(jnp.abs(up_vals))
    top_down = jnp.max(jnp.abs(down_vals))
    peak_qkv, peak_proj, peak_up, peak_down = lax.pmax(
        (top_qkv, top_proj, top_up, top_down), "tensor"
    )
    peak_tokens = lax.pmax(jnp.max(jnp.abs(token_vals)), ("dp", "tensor"))
    token_ints, step_tokens = quantize(token_vals, peak_tokens)
    qkv_ints, step_qkv = quantize(qkv_vals, peak_qkv[:, None, None])
    proj_ints, step_proj = quantize(proj_vals, peak_proj)
    up_ints, step_up = quantize(up_vals, peak_up)
    down_ints, step_down = quantize(down_vals, peak_down)
    qkv_low = qkv_ints.astype(jnp.bfloat16)
    proj_low = proj_ints.astype(jnp.bfloat16)
    up_low = up_ints.astype(jnp.bfloat16)
    down_low = down_ints.astype(jnp.bfloat16)
    group_tokens = group_rows(token_ints.astype(jnp.bfloat16))
    total_rows = group_tokens.shape[0]
    qkv_raw = jnp.einsum("td,idh->ith", group_tokens, qkv_low, preferred_element_type=jnp.float32)
    qkv_out = qkv_raw * (step_tokens * step_qkv)
    bias_vals = qv_bias.astype(jnp.float32)
    pair_shape = (rows_here // 2, 2, seq_len, heads_here, HEAD_DIM)
    queries = (qkv_out[0] + bias_vals[0]).astype(jnp.bfloat16).reshape(pair_shape)
    keys_low = qkv_out[1].astype(jnp.bfloat16).reshape(pair_shape)
    values_low = (qkv_out[2] + bias_vals[1]).astype(jnp.bfloat16).reshape(pair_shape)
    pair_segments = segment_ids.reshape(rows_here // 2, 2, seq_len)
    pair_lengths = row_lengths.reshape(rows_here // 2, 2)
    context_pairs, log_totals = lax.map(
        attend_pair, (queries, keys_low, values_low, pair_segments, pair_lengths)
    )
    context_low = context_pairs.reshape(total_rows, heads_here * HEAD_DIM).astype(jnp.bfloat16)

    def proj_term(row_start, row_count):
        return jnp.dot(context_low, proj_low, preferred_element_type=jnp.float32)

    proj_raw = reduce_rows(proj_term, own_rows)
    first_in = token_vals + (proj_raw * step_proj + proj_bias.astype(jnp.float32))
    first_gain_vals = first_gain.astype(jnp.float32)
    normed, first_standard, first_inverse = norm_forward(
        first_in, first_gain_vals, first_shift.astype(jnp.float32)
    )
    normed_low = normed.astype(jnp.bfloat16)
    up_full, up_bias_full, down_full = (
        lax.all_gather(up_low, "tensor", axis=1, tiled=True),
        lax.all_gather(up_bias, "tensor", axis=0, tiled=True),
        lax.all_gather(down_low, "tensor", axis=0, tiled=True),
    )
    pre_act = jnp.dot(
        normed_low, up_full, preferred_element_type=jnp.float32
    ) * step_up + up_bias_full.astype(jnp.float32)
    activated, gelu_pull = jax.vjp(exact_gelu, pre_act)
    act_low = activated.astype(jnp.bfloat16)
    down_raw = jnp.dot(act_low, down_full, preferred_element_type=jnp.float32)
    second_in = normed + (down_raw * step_down + down_bias.astype(jnp.float32))
    second_gain_vals = second_gain.astype(jnp.float32)
    layer_out, second_standard, second_inverse = norm_forward(
        second_in, second_gain_vals, second_shift.astype(jnp.float32)
    )
    grad_second, second_gain_grad, second_shift_grad = norm_backward(
        out_grad.astype(jnp.float32), second_standard, second_inverse, second_gain_vals
    )
    down_bias_grad = jnp.sum(grad_second, axis=0)
    grad_down = (grad_second * step_down).astype(jnp.bfloat16)
    down_full_grad = jnp.einsum("tf,td->fd", act_low, grad_down, preferred_element_type=jnp.float32)
    act_grad = jnp.einsum("td,fd->tf", grad_down, down_full, preferred_element_type=jnp.float32)
    (pre_grad,) = gelu_pull(act_grad)
    up_bias_full_grad = jnp.sum(pre_grad, axis=0)
    grad_up = (pre_grad * step_up).astype(jnp.bfloat16)
    up_full_grad = jnp.einsum("td,tf->df", normed_low, grad_up, preferred_element_type=jnp.float32)
    normed_back = jnp.einsum("tf,df->td", grad_up, up_full, preferred_element_type=jnp.float32)
    up_int_grad, up_bias_grad, down_int_grad = (
        lax.psum_scatter(
            up_full_grad.astype(jnp.bfloat16), "tensor", scatter_dimension=1, tiled=True
        ).astype(jnp.float32),
        lax.psum_scatter(
            up_bias_full_grad.astype(jnp.bfloat16), "tensor", scatter_dimension=0, tiled=True
        ).astype(jnp.float32),
        lax.psum_scatter(
            down_full_grad.astype(jnp.bfloat16), "tensor", scatter_dimension=0, tiled=True
        ).astype(jnp.float32),
    )
    grad_normed = grad_second + normed_back
    grad_first, first_gain_grad, first_shift_grad = norm_backward(
        grad_normed, first_standard, first_inverse, first_gain_vals
    )
    proj_bias_grad = jnp.sum(grad_first, axis=0)
    grad_proj = (grad_first * step_proj).astype(jnp.bfloat16)
    group_grad = group_rows(grad_proj)
    proj_int_grad = jnp.einsum(
        "tc,td->cd", context_low, group_grad, preferred_element_type=jnp.float32
    )
    grad_context = jnp.einsum(
        "td,cd->tc", group_grad, proj_low, preferred_element_type=jnp.float32
    ).astype(jnp.bfloat16)
    grad_pairs = lax.map(
        attend_back,
        (
            queries,
            keys_low,
            values_low,
            pair_segments,
            pair_lengths,
            log_totals,
            grad_context.reshape(pair_shape),
        ),
    )
    grad_queries = grad_pairs[0].reshape(total_rows, heads_here * HEAD_DIM)
    grad_keys = grad_pairs[1].reshape(total_rows, heads_here * HEAD_DIM)
    grad_values = grad_pairs[2].reshape(total_rows, heads_here * HEAD_DIM)
    qv_bias_grad = jnp.stack([jnp.sum(grad_queries, axis=0), jnp.sum(grad_values, axis=0)])
    grad_qkv = (
        jnp.stack([grad_queries, grad_keys, grad_values]) * (step_tokens * step_qkv)
    ).astype(jnp.bfloat16)
    qkv_int_grad = jnp.einsum(
        "td,ith->idh", group_tokens, grad_qkv, preferred_element_type=jnp.float32
    )

    def input_term(row_start, row_count):
        return jnp.einsum("ith,idh->td", grad_qkv, qkv_low, preferred_element_type=jnp.float32)

    token_int_grad = reduce_rows(input_term, own_rows)
    tokens_grad = grad_first + token_int_grad * passes(token_vals) / step_tokens
    shard_sums = (
        lax.psum(qkv_int_grad.astype(jnp.bfloat16), "dp").astype(jnp.float32),
        lax.psum(qv_bias_grad.astype(jnp.bfloat16), "dp").astype(jnp.float32),
        lax.psum(proj_int_grad.astype(jnp.bfloat16), "dp").astype(jnp.float32),
        lax.psum(up_int_grad.astype(jnp.bfloat16), "dp").astype(jnp.float32),
        lax.psum(up_bias_grad.astype(jnp.bfloat16), "dp").astype(jnp.float32),
        lax.psum(down_int_grad.astype(jnp.bfloat16), "dp").astype(jnp.float32),
    )
    common_sums = lax.psum(
        (
            proj_bias_grad,
            first_gain_grad,
            first_shift_grad,
            down_bias_grad,
            second_gain_grad,
            second_shift_grad,
        ),
        ("dp", "tensor"),
    )
    return (
        layer_out.astype(jnp.bfloat16),
        tokens_grad,
        shard_sums[0] * passes(qkv_vals) / step_qkv,
        shard_sums[1],
        shard_sums[2] * passes(proj_vals) / step_proj,
        common_sums[0],
        common_sums[1],
        common_sums[2],
        shard_sums[3] * passes(up_vals) / step_up,
        shard_sums[4],
        shard_sums[5] * passes(down_vals) / step_down,
        common_sums[3],
        common_sums[4],
        common_sums[5],
    )


def solution(mesh):
    in_specs = (
        P(("dp", "tensor"), None),
        P("dp", None),
        P("dp"),
        P(None, None, "tensor"),
        P(None, "tensor"),
        P("tensor", None),
        P(),
        P(),
        P(),
        P(None, "tensor"),
        P("tensor"),
        P("tensor", None),
        P(),
        P(),
        P(),
        P(("dp", "tensor"), None),
    )
    out_specs = (
        P(("dp", "tensor"), None),
        P(("dp", "tensor"), None),
        P(None, None, "tensor"),
        P(None, "tensor"),
        P("tensor", None),
        P(),
        P(),
        P(),
        P(None, "tensor"),
        P("tensor"),
        P("tensor", None),
        P(),
        P(),
        P(),
    )
    return jax.shard_map(local, mesh=mesh, in_specs=in_specs, out_specs=out_specs, check_vma=False)
```

profile of v0, /device:TPU:0, one launch (start us, length us, event | category | flops | bytes accessed | tf_op | source)
XLA Modules:
  0.0 994.4 jit_solution(8438317445170648339)
XLA Ops:
  9.8 42.2 %pmax.36 = f32[]{:T(128)} all-reduce(f32[]{:T(128)} %fusion.88), channel_id=1, replica_groups=mesh['dp'=8,'tensor'=4] {'dp','tensor'}, use_global_device_ids=true, to_apply=%region_3.0 | all-reduce | flops 1 | bytes 8 | tf_op jit(solution)/shard_map/pmax | solution.py:145
  59.2 6.6 all-reduce.2
  69.5 46.4 %all-gather.6.cloned.1.call-done = bf16[8192,512]{1,0:T(8,128)(2,1)} async-done(((bf16[2048,512]{1,0:T(8,128)(2,1)}), bf16[8192,512]{1,0:T(8,128)(2,1)}) %all-gather.6.cloned.1.call-update) | async-done | bytes 8388624 | tf_op jit(solution)/shard_map/all_gather | solution.py:27
  115.9 6.2 multiply_bitcast_fusion
  127.6 6.6 squeeze.37
  134.2 6.6 squeeze.38
  156.7 59.9 %while.28 = (s32[]{:T(128)}, bf16[8,2,512,2,64]{2,4,3,1,0:T(8,128)(2,1)S(1)}, f32[8,2,2,512,1]{3,2,1,4,0:T(2,128)}, bf16[8,2,512,2,64]{2,4,3,1,0:T(8,128)(2,1)},...) while((s32[]{:T(128)}, ...), condition=%wide.region_7.0_spmd.clone, body=%wide.region_4.7_spmd.sunk.clone | while | flops 282852352 | bytes 16597121 | solution.py:166
  238.7 62.4 %reduce-scatter.5.cloned.1.call-done = bf16[2048,512]{1,0:T(8,128)(2,1)} async-done(((bf16[8192,512]{1,0:T(8,128)(2,1)}), bf16[2048,512]{1,0:T(8,128)(2,1)}) %reduce-scatter.5.cloned.1.call-update) | async-done | bytes 2097168 | tf_op jit(solution)/shard_map/reduce_scatter | solution.py:31
  305.1 20.9 %all-gather.8.cloned.1.call-done = bf16[512,2048]{1,0:T(8,128)(2,1)} async-done(((bf16[512,512]{1,0:T(8,128)(2,1)}), bf16[512,2048]{1,0:T(8,128)(2,1)}) %all-gather.8.cloned.1.call-update) | async-done | bytes 2097168 | tf_op jit(solution)/shard_map/all_gather | solution.py:182
  325.9 45.9 %multiply_convert_fusion.2 = (bf16[2048,2048]{1,0:T(8,128)(2,1)}, f32[2048,2048]{1,0:T(8,128)}, f32[2048,2048]{1,0:T(8,128)}) fusion(f32[2048]{0:T(1024)S(1)} %bitcast.166, f32[]{:T(128)S(6)} %div.112, bf16[512,2048]{1,0:T(8,128)(2,1)} %all-gather.8.cloned.1.call-done, f32[512]{0:T(512)S(1)} %convert_element_type.180, f32[512]{0:T(512)S(1)} %convert_element_type.179, ...), kind=kOutput, calls=%fused_computation.79 | convolution fusion | flops 4586471424 | bytes 48265224 | tf_op jit(solution)/shard_map/dot_general | solution.py:186
  371.9 9.0 fusion.133
  390.3 22.4 %fusion.134 = (bf16[2048]{0:T(1024)(128)(2,1)S(1)}, f32[2048,2048]{1,0:T(8,128)}) fusion(f32[2048,2048]{1,0:T(8,128)} %get-tuple-element.289, bf16[2048,512]{1,0:T(8,128)(2,1)} %all-gather.10.cloned.1.call-done, f32[2048,512]{1,0:T(8,128)} %get-tuple-element.285, f32[]{:T(128)S(6)} %div.115, f32[2048]{0:T(1024)S(1)} %bitcast.167, ...), kind=kOutput, calls=%fused_computation.200 | convolution fusion | flops 4364171264 | bytes 56635400 | tf_op jit(solution)/shard_map/td,fd->tf/dot_general | solution.py:203
  412.7 11.7 %multiply_reduce_fusion.1 = (f32[512]{0:T(512)S(1)}, f32[2048]{0:T(1024)S(1)}, f32[2048]{0:T(1024)S(1)}, f32[512]{0:T(512)S(1)}, f32[2048,512]{1,0:T(8,128)S(1)}) fusion(f32[2048]{0:T(1024)S(1)} %add_rsqrt_fusion.1, f32[2048]{0:T(1024)S(1)} %broadcast_multiply_fusion.5, f32[512]{0:T(512)S(1)} %convert_element_type.178, f32[]{:T(128)S(6)} %div.107, ...), kind=kOutput, calls=%fused_computation.126 | convolution fusion | flops 4319079424 | bytes 31498248 | tf_op jit(solution)/shard_map/tf,df->td/dot_general | solution.py:208
  430.8 13.4 %fusion.99 = bf16[512,2048]{1,0:T(8,128)(2,1)} fusion(f32[2048,2048]{1,0:T(8,128)} %get-tuple-element.302, f32[]{:T(128)S(6)} %div.112, f32[512]{0:T(512)S(1)} %convert_element_type.180, f32[512]{0:T(512)S(1)} %convert_element_type.179, bf16[2048,512]{1,0:T(8,128)(2,1)} %reduce-scatter.5.cloned.1.call-done, bf16[2048,512]{1,0:T(8,128)(2,1)S(1)} %copy-done, ...), kind=kOutput, calls=%fused_computation.145 | convolution fusion | flops 4314890240 | bytes 23091208 | tf_op jit(solution)/shard_map/td,tf->df/dot_general | solution.py:207
  444.3 10.5 %convolution_convert_fusion.2 = bf16[2048,512]{1,0:T(8,128)(2,1)} fusion(bf16[2048,2048]{1,0:T(8,128)(2,1)} %get-tuple-element.288, f32[2048,512]{1,0:T(8,128)} %get-tuple-element.285, f32[]{:T(128)S(6)} %div.115), kind=kOutput, calls=%fused_computation.144 | convolution fusion | flops 4298113024 | bytes 14680068 | tf_op jit(solution)/shard_map/tf,td->fd/dot_general | solution.py:202
  454.9 34.1 %all-gather.12.cloned.1.call-done = bf16[8192,512]{1,0:T(8,128)(2,1)} async-done(((bf16[2048,512]{1,0:T(8,128)(2,1)}), bf16[8192,512]{1,0:T(8,128)(2,1)}) %all-gather.12.cloned.1.call-update) | async-done | bytes 8388624 | tf_op jit(solution)/shard_map/all_gather | solution.py:27
  489.0 7.1 convolution_convert_fusion.1
  496.1 8.6 reshape.233
  504.8 10.6 %copy.72 = bf16[8,2,512,2,64]{2,4,3,1,0:T(8,128)(2,1)} copy(bf16[8,2,512,2,64]{4,3,2,1,0:T(2,128)(2,1)} %reshape.233) | data formatting | bytes 4194304 | tf_op jit(solution)/shard_map/while | solution.py:233
  515.4 250.8 %while.29 = (s32[]{:T(128)}, f32[8,2,512,2,64]{2,4,3,1,0:T(8,128)}, f32[8,2,512,2,64]{2,1,0,4,3:T(2,128)}, f32[8,2,512,2,64]{2,4,3,1,0:T(8,128)}, bf16[8,2,512,2...) while((s32[]{:T(128)}, f32[8,2,512,2,64]{2,4,3,1,0:T(8,128)}, ...), condition=%wide.region_25.26_spmd.clone, body=%wide.region_23.25_spmd.sunk.clone | while | flops 687609856 | bytes 52209824 | solution.py:233
  526.4 8.4 fusion.202
  534.8 7.2 fusion.203
  558.2 8.1 fusion.202
  566.3 7.1 fusion.203
  589.6 8.0 fusion.202
  597.6 7.1 fusion.203
  620.8 8.0 fusion.202
  628.8 7.1 fusion.203
  652.1 8.1 fusion.202
  660.1 7.1 fusion.203
  683.4 8.1 fusion.202
  691.4 7.1 fusion.203
  714.7 8.0 fusion.202
  722.7 7.1 fusion.203
  745.9 8.0 fusion.202
  753.9 7.1 fusion.203
  766.2 7.4 copy.75
  773.6 6.6 stack_reshape.11
  780.2 6.8 stack_reshape.10
  786.9 7.3 copy.73
  794.3 6.6 stack_reshape.9
  808.7 7.6 fusion.104
  816.4 10.3 %bitcast_convert_fusion = bf16[8192,512]{1,0:T(8,128)(2,1)} fusion(bf16[3,512,128]{1,2,0:T(8,128)(2,1)S(1)} %copy-done.9, f32[3]{0:T(128)S(1)} %copy-done.23, f32[1,8192,128]{1,2,0:T(8,128)} %stack_reshape.11, f32[1,8192,128]{1,2,0:T(8,128)} %stack_reshape.10, f32[1,8192,128]{1,2,0:T(8,128)} %stack_reshape.9, f32[3]{0:T(128)S(1)} %copy-done.27), kind=kOutput, calls=%fused_computation.76 | convolution fusion | flops 3239575552 | bytes 21364760 | tf_op jit(solution)/shard_map/ith,idh->td/dot_general | solution.py:257
  828.5 6.5 all-reduce
  835.1 40.9 %all-reduce.1 = (f32[512]{0:T(512)}, f32[512]{0:T(512)}, f32[512]{0:T(512)}, f32[512]{0:T(512)}, f32[512]{0:T(512)}, /*index=5*/f32[512]{0:T(512)}) all-reduce(f32[512]{0:T(512)S(1)} %get-tuple-element.286, f32[512]{0:T(512)S(1)} %get-tuple-element.220, ...), channel_id=1, replica_groups=mesh['dp'=8,'tensor'=4] {'dp','tensor'}, use_global_device_ids=true, to_apply=%region_33.34 | all-reduce | flops 3072 | bytes 24576 | tf_op jit(solution)/shard_map/psum | solution.py:269
  882.5 22.2 %all-reduce.3 = (bf16[2,128]{1,0:T(2,128)(2,1)}, bf16[512]{0:T(512)(128)(2,1)S(1)}) all-reduce(bf16[2,128]{1,0:T(2,128)(2,1)S(1)} %pad_maximum_fusion, bf16[512]{0:T(512)(128)(2,1)S(1)} %dynamic-slice.1), channel_id=1, replica_groups=mesh['dp'=8,'tensor'=4] {'dp'}, use_global_device_ids=true, to_apply=%region_30.31 | all-reduce | flops 768 | bytes 3072 | tf_op jit(solution)/shard_map/psum | solution.py:263
  918.1 62.9 %reduce-scatter.7.cloned.1.call-done = bf16[2048,512]{1,0:T(8,128)(2,1)} async-done(((bf16[8192,512]{1,0:T(8,128)(2,1)}), bf16[2048,512]{1,0:T(8,128)(2,1)}) %reduce-scatter.7.cloned.1.call-update) | async-done | bytes 2097168 | tf_op jit(solution)/shard_map/reduce_scatter | solution.py:31
  981.0 6.6 fusion.92
  (324 shorter events, 290.3 us)
Async XLA Ops:
  7.2 50.3 %copy-start.20 = (bf16[3,512,128]{2,1,0:T(8,128)(2,1)S(1)}, bf16[3,512,128]{2,1,0:T(8,128)(2,1)}, u32[]{:S(2)}) copy-start(bf16[3,512,128]{2,1,0:T(8,128)(2,1)} %param.23) | copy-start | bytes 1179652
  7.2 50.5 %copy-start.17 = (bf16[128,512]{1,0:T(8,128)(2,1)S(1)}, bf16[128,512]{1,0:T(8,128)(2,1)}, u32[]{:S(2)}) copy-start(bf16[128,512]{1,0:T(8,128)(2,1)} %param.25) | copy-start | bytes 393220
  7.2 108.7 %all-gather.6.cloned.1.call-start = ((), (), s32[]{:S(2)}) async-start(), calls=%async_computation.4 | async-start | bytes 10485760 | tf_op jit(solution)/shard_map/all_gather | solution.py:27
  9.8 48.7 %copy-start.10 = (bf16[512,512]{1,0:T(8,128)(2,1)S(1)}, bf16[512,512]{1,0:T(8,128)(2,1)}, u32[]{:S(2)}) copy-start(bf16[512,512]{1,0:T(8,128)(2,1)} %param.29) | copy-start | bytes 1572868
  9.8 48.7 %copy-start.12 = (bf16[512,512]{1,0:T(8,128)(2,1)S(1)}, bf16[512,512]{1,0:T(8,128)(2,1)}, u32[]{:S(2)}) copy-start(bf16[512,512]{1,0:T(8,128)(2,1)} %param.31) | copy-start | bytes 1572868
  52.6 13.9 %copy-start.39 = (bf16[2,128]{1,0:T(2,128)(2,1)S(1)}, bf16[2,128]{1,0:T(2,128)(2,1)}, u32[]{:S(2)}) copy-start(bf16[2,128]{1,0:T(2,128)(2,1)} %param.24) | copy-start | bytes 1540
  52.6 14.0 %copy-start.21 = (s32[16,512]{1,0:T(8,128)S(1)}, s32[16,512]{1,0:T(8,128)}, u32[]{:S(2)}) copy-start(s32[16,512]{1,0:T(8,128)} %param.21) | copy-start | bytes 98308
  52.6 14.6 %copy-start.38 = (s32[16]{0:T(128)S(1)}, s32[16]{0:T(128)}, u32[]{:S(2)}) copy-start(s32[16]{0:T(128)} %param.22) | copy-start | bytes 196
  57.4 243.7 %reduce-scatter.5.cloned.1.call-start = ((), (), s32[]{:S(2)}) async-start(), calls=%async_computation.5 | async-start | bytes 10485760 | tf_op jit(solution)/shard_map/reduce_scatter | solution.py:31
  57.7 64.4 %copy-start.8 = (bf16[3,512,128]{1,2,0:T(8,128)(2,1)}, bf16[3,512,128]{1,2,0:T(8,128)(2,1)S(1)}, u32[]{:S(2)}) copy-start(bf16[3,512,128]{1,2,0:T(8,128)(2,1)S(1)} %copy.65) | copy-start | bytes 1179652
  69.5 52.6 %copy-start.22 = (f32[3]{0:T(128)}, f32[3]{0:T(128)S(1)}, u32[]{:S(2)}) copy-start(f32[3]{0:T(128)S(1)} %get-tuple-element.295) | copy-start | bytes 40
  69.5 52.6 %copy-start.26 = (f32[3]{0:T(128)}, f32[3]{0:T(128)S(1)}, u32[]{:S(2)}) copy-start(f32[3]{0:T(128)S(1)} %get-tuple-element.296) | copy-start | bytes 40
  145.2 4.2 copy-start.5
  149.5 3.6 copy-start.6
  149.5 3.6 copy-start.37
  216.6 6.8 copy-start.29
  216.6 6.8 copy-start.18
  223.4 5.7 copy-start.2
  229.1 4.2 copy-start.30
  229.1 4.3 copy-start.31
  229.1 9.5 copy-start.32
  229.1 9.5 copy-start.33
  229.1 9.5 copy-start.34
  229.1 9.5 copy-start.35
  229.1 9.5 copy-start.36
  229.1 71.9 %copy-start = (bf16[2048,512]{1,0:T(8,128)(2,1)S(1)}, bf16[2048,512]{1,0:T(8,128)(2,1)}, u32[]{:S(2)}) copy-start(bf16[2048,512]{1,0:T(8,128)(2,1)} %param.20) | copy-start | bytes 6291460
  229.2 96.8 %all-gather.8.cloned.1.call-start = ((), (), s32[]{:S(2)}) async-start(), calls=%async_computation.6 | async-start | bytes 2621440 | tf_op jit(solution)/shard_map/all_gather | solution.py:182
  231.3 140.6 %all-gather.10.cloned.1.call-start = ((), (), s32[]{:S(2)}) async-start(), calls=%async_computation.7 | async-start | bytes 2621440 | tf_op jit(solution)/shard_map/all_gather | solution.py:184
  233.3 255.7 %all-gather.12.cloned.1.call-start = ((), (), s32[]{:S(2)}) async-start(), calls=%async_computation.8 | async-start | bytes 10485760 | tf_op jit(solution)/shard_map/all_gather | solution.py:27
  301.1 2.6 copy-start.3
  412.7 11.7 %copy-start.4 = (bf16[2048,512]{1,0:T(8,128)(2,1)S(1)}, bf16[2048,512]{1,0:T(8,128)(2,1)}, u32[]{:S(2)}) copy-start(bf16[2048,512]{1,0:T(8,128)(2,1)} %reduce-scatter.5.cloned.1.call-done) | copy-start | bytes 6291460
  426.7 2.0 copy-start.1
  430.6 385.7 %reduce-scatter.9.cloned.1.call-start = ((), (), s32[]{:S(2)}) async-start(), calls=%async_computation.10 | async-start | bytes 2621440 | tf_op jit(solution)/shard_map/reduce_scatter | solution.py:210
  444.2 372.1 %reduce-scatter.11.cloned.1.call-start = ((), (), s32[]{:S(2)}) async-start(), calls=%async_computation.11 | async-start | bytes 2621440 | tf_op jit(solution)/shard_map/reduce_scatter | solution.py:216
  444.3 44.7 %copy-start.19 = (bf16[128,512]{1,0:T(8,128)(2,1)S(1)}, bf16[128,512]{1,0:T(8,128)(2,1)}, u32[]{:S(2)}) copy-start(bf16[128,512]{1,0:T(8,128)(2,1)} %param.25) | copy-start | bytes 393220
  454.8 452.2 %all-reduce.7.cloned.1.call-start = ((), (), s32[]{:S(2)}) async-start(), calls=%async_computation.12 | async-start | bytes 3145728 | tf_op jit(solution)/shard_map/psum | solution.py:262
  800.9 6.1 copy-start.14
  800.9 6.5 copy-start.15
  800.9 7.7 copy-start.16
  800.9 7.7 copy-start.27
  808.7 7.7 copy-start.9
  808.7 7.7 copy-start.23
  816.3 164.7 %reduce-scatter.7.cloned.1.call-start = ((), (), s32[]{:S(2)}) async-start(), calls=%async_computation.9 | async-start | bytes 10485760 | tf_op jit(solution)/shard_map/reduce_scatter | solution.py:31
  826.6 8.5 copy-start.24
  826.6 8.5 copy-start.25
  826.7 8.5 copy-start.28
  878.5 34.7 %copy-start.11 = (bf16[512,512]{1,0:T(8,128)(2,1)S(1)}, bf16[512,512]{1,0:T(8,128)(2,1)}, u32[]{:S(2)}) copy-start(bf16[512,512]{1,0:T(8,128)(2,1)} %param.29) | copy-start | bytes 1572868
  878.5 37.1 %copy-start.13 = (bf16[512,512]{1,0:T(8,128)(2,1)S(1)}, bf16[512,512]{1,0:T(8,128)(2,1)}, u32[]{:S(2)}) copy-start(bf16[512,512]{1,0:T(8,128)(2,1)} %param.31) | copy-start | bytes 1572868
  (2 other events, 2.2 us)
Sparse Core Ops, SparseCore 0:
  57.6 58.2 all-gather.5
  229.3 71.7 reduce-scatter.4
  303.3 22.5 all-gather.7
  328.0 22.5 all-gather.9
  430.7 58.2 all-gather.11
  491.5 31.4 reduce-scatter.8
  525.5 31.4 reduce-scatter.10
  816.4 90.5 all-reduce.6
  909.8 71.1 reduce-scatter.6
where the time goes:
time: 1000 us; the launch traced here: 994 us
  matrix products  409 us (41%)
  waiting for transfers between devices  227 us (23%)
  local copies, waits for them, and re-layouts  131 us (13%)
  blocking collectives  124 us (12%)
  other arithmetic  84.1 us (8%)
  between operations  18.7 us (2%)
    reduce_scatter x2, waiting for transfers between devices, reduce_rows(): lax.psum_scatter(term_fn(jnp.int32(0), lax.axis_size('tensor') * own_rows...  125 us
    all_gather x2, waiting for transfers between devices, group_rows(): return lax.all_gather(values, 'tensor', axis=0, tiled=True)  80.5 us
    dot_general x8, matrix products, attend_back(): jnp.einsum('rhqk,rkhe->rqhe', grad_scores, keys_low, preferred_element_ty...  64.8 us
    dot_general x8, matrix products, attend_back(): jnp.einsum('rhqk,rqhe->rkhe', grad_scores, queries, preferred_element_typ...  57 us
    dot_general x16, matrix products, pair_scores(): jnp.einsum('rqhe,rkhe->rhqk', queries, keys_low, preferred_element_type=j...  51.8 us
    dot_general x1, matrix products, local(): jnp.dot(normed_low, up_full, preferred_element_type=jnp.float32) * step_up  45.9 us
    pmax x1, blocking collectives, local(): peak_tokens = lax.pmax(jnp.max(jnp.abs(token_vals)), ('dp', 'tensor'))  42.2 us
    psum x1, blocking collectives, local(): lax.psum((proj_bias_grad, first_gain_grad, first_shift_grad, down_bias_gr...  40.9 us
  transfers between devices with their start and end apart: 9, of which 6 were waited for; matrix products, arithmetic and copies ran while one was open for 44% of the time, Pallas kernels for 0%

commit v1 on v0

--- a/solution.py
+++ b/solution.py
@@ -266,17 +266,16 @@
         lax.psum(up_bias_grad.astype(jnp.bfloat16), "dp").astype(jnp.float32),
         lax.psum(down_int_grad.astype(jnp.bfloat16), "dp").astype(jnp.float32),
     )
-    common_sums = lax.psum(
-        (
-            proj_bias_grad,
-            first_gain_grad,
-            first_shift_grad,
-            down_bias_grad,
-            second_gain_grad,
-            second_shift_grad,
-        ),
-        ("dp", "tensor"),
-    )
+    common_sums = (
+        proj_bias_grad,
+        first_gain_grad,
+        first_shift_grad,
+        down_bias_grad,
+        second_gain_grad,
+        second_shift_grad,
+    )
+    for axis in ("tensor", "dp"):
+        common_sums = lax.psum(common_sums, axis)
     return (
         layer_out.astype(jnp.bfloat16),
         tokens_grad,

time: 1000 us -> 1000 us (level)
    psum x1 -> x2, blocking collectives: 40.9 us -> 48.1 us  [local(): common_sums = lax.psum(common_sums, axis)]
  transfers between devices with their start and end apart: 9 -> 9, of which waited for: 6 -> 5; matrix products, arithmetic and copies ran while one was open for 44% -> 44% of each run, Pallas kernels for 0% -> 0%
where the time goes in v1:
time: 1000 us; the launch traced here: 993 us
  matrix products  415 us (42%)
  waiting for transfers between devices  224 us (22%)
  blocking collectives  127 us (13%)
  local copies, waits for them, and re-layouts  122 us (12%)
  other arithmetic  85.4 us (9%)
  between operations  18.7 us (2%)
    reduce_scatter x2, waiting for transfers between devices, reduce_rows(): lax.psum_scatter(term_fn(jnp.int32(0), lax.axis_size('tensor') * own_rows...  122 us
    all_gather x2, waiting for transfers between devices, group_rows(): return lax.all_gather(values, 'tensor', axis=0, tiled=True)  80.9 us
    dot_general x8, matrix products, attend_back(): jnp.einsum('rhqk,rkhe->rqhe', grad_scores, keys_low, preferred_element_ty...  64.8 us
    dot_general x8, matrix products, attend_back(): jnp.einsum('rhqk,rqhe->rkhe', grad_scores, queries, preferred_element_typ...  57 us
    dot_general x16, matrix products, pair_scores(): jnp.einsum('rqhe,rkhe->rhqk', queries, keys_low, preferred_element_type=j...  51.8 us
    psum x2, blocking collectives, local(): common_sums = lax.psum(common_sums, axis)  48.1 us
    dot_general x1, matrix products, local(): jnp.dot(normed_low, up_full, preferred_element_type=jnp.float32) * step_up  46 us
    pmax x1, blocking collectives, local(): peak_tokens = lax.pmax(jnp.max(jnp.abs(token_vals)), ('dp', 'tensor'))  42.2 us
  transfers between devices with their start and end apart: 9, of which 5 were waited for; matrix products, arithmetic and copies ran while one was open for 44% of the time, Pallas kernels for 0%

profile of v1, /device:TPU:0, one launch (start us, length us, event | category | flops | bytes accessed | tf_op | source)
XLA Modules:
  0.0 993.1 jit_solution(2691219919417635453)
XLA Ops:
  9.8 42.2 %pmax.36 = f32[]{:T(128)} all-reduce(f32[]{:T(128)} %fusion.88), channel_id=1, replica_groups=mesh['dp'=8,'tensor'=4] {'dp','tensor'}, use_global_device_ids=true, to_apply=%region_3.0 | all-reduce | flops 1 | bytes 8 | tf_op jit(solution)/shard_map/pmax | solution.py:145
  59.2 6.6 all-reduce.3
  69.1 46.8 %all-gather.6.cloned.1.call-done = bf16[8192,512]{1,0:T(8,128)(2,1)} async-done(((bf16[2048,512]{1,0:T(8,128)(2,1)}), bf16[8192,512]{1,0:T(8,128)(2,1)}) %all-gather.6.cloned.1.call-update) | async-done | bytes 8388624 | tf_op jit(solution)/shard_map/all_gather | solution.py:27
  126.3 6.6 squeeze.37
  132.9 6.6 squeeze.38
  153.6 60.1 %while.28 = (s32[]{:T(128)}, bf16[8,2,512,2,64]{2,4,3,1,0:T(8,128)(2,1)}, f32[8,2,2,512,1]{3,2,1,4,0:T(2,128)}, bf16[8,2,512,2,64]{2,4,3,1,0:T(8,128)(2,1)}, s32...) while((s32[]{:T(128)}, ...), condition=%wide.region_7.0_spmd.clone, body=%wide.region_4.7_spmd.sunk.clone | while | flops 282852352 | bytes 16597121 | solution.py:166
  237.4 62.4 %reduce-scatter.5.cloned.1.call-done = bf16[2048,512]{1,0:T(8,128)(2,1)} async-done(((bf16[8192,512]{1,0:T(8,128)(2,1)}), bf16[2048,512]{1,0:T(8,128)(2,1)}) %reduce-scatter.5.cloned.1.call-update) | async-done | bytes 2097168 | tf_op jit(solution)/shard_map/reduce_scatter | solution.py:31
  303.8 20.9 %all-gather.8.cloned.1.call-done = bf16[512,2048]{1,0:T(8,128)(2,1)} async-done(((bf16[512,512]{1,0:T(8,128)(2,1)}), bf16[512,2048]{1,0:T(8,128)(2,1)}) %all-gather.8.cloned.1.call-update) | async-done | bytes 2097168 | tf_op jit(solution)/shard_map/all_gather | solution.py:182
  324.6 46.0 %multiply_convert_fusion.2 = (bf16[2048,2048]{1,0:T(8,128)(2,1)}, f32[2048,2048]{1,0:T(8,128)}, f32[2048,2048]{1,0:T(8,128)}) fusion(f32[2048]{0:T(1024)S(1)} %bitcast.166, f32[]{:T(128)S(6)} %div.112, bf16[512,2048]{1,0:T(8,128)(2,1)} %all-gather.8.cloned.1.call-done, f32[512]{0:T(512)S(1)} %convert_element_type.180, f32[512]{0:T(512)S(1)} %convert_element_type.179, ...), kind=kOutput, calls=%fused_computation.79 | convolution fusion | flops 4586471424 | bytes 48265224 | tf_op jit(solution)/shard_map/dot_general | solution.py:186
  370.6 9.0 fusion.133
  389.0 22.4 %fusion.134 = (bf16[2048]{0:T(1024)(128)(2,1)S(1)}, f32[2048,2048]{1,0:T(8,128)}) fusion(f32[2048,2048]{1,0:T(8,128)} %get-tuple-element.295, bf16[2048,512]{1,0:T(8,128)(2,1)} %all-gather.10.cloned.1.call-done, f32[2048,512]{1,0:T(8,128)} %get-tuple-element.291, f32[]{:T(128)S(6)} %div.115, f32[2048]{0:T(1024)S(1)} %bitcast.167, ...), kind=kOutput, calls=%fused_computation.200 | convolution fusion | flops 4364171264 | bytes 56635400 | tf_op jit(solution)/shard_map/td,fd->tf/dot_general | solution.py:203
  411.4 11.7 %multiply_reduce_fusion.1 = (f32[512]{0:T(512)S(1)}, f32[2048]{0:T(1024)S(1)}, f32[2048]{0:T(1024)S(1)}, f32[512]{0:T(512)S(1)}, f32[2048,512]{1,0:T(8,128)S(1)}) fusion(f32[2048]{0:T(1024)S(1)} %add_rsqrt_fusion.1, f32[2048]{0:T(1024)S(1)} %broadcast_multiply_fusion.5, f32[512]{0:T(512)S(1)} %convert_element_type.178, f32[]{:T(128)S(6)} %div.107, ...), kind=kOutput, calls=%fused_computation.126 | convolution fusion | flops 4319079424 | bytes 31498248 | tf_op jit(solution)/shard_map/tf,df->td/dot_general | solution.py:208
  429.6 13.4 %fusion.99 = bf16[512,2048]{1,0:T(8,128)(2,1)} fusion(f32[2048,2048]{1,0:T(8,128)} %get-tuple-element.308, f32[]{:T(128)S(6)} %div.112, f32[512]{0:T(512)S(1)} %convert_element_type.180, f32[512]{0:T(512)S(1)} %convert_element_type.179, bf16[2048,512]{1,0:T(8,128)(2,1)} %reduce-scatter.5.cloned.1.call-done, bf16[2048,512]{1,0:T(8,128)(2,1)S(1)} %copy-done, ...), kind=kOutput, calls=%fused_computation.145 | convolution fusion | flops 4314890240 | bytes 23091208 | tf_op jit(solution)/shard_map/td,tf->df/dot_general | solution.py:207
  443.1 10.5 %convolution_convert_fusion.2 = bf16[2048,512]{1,0:T(8,128)(2,1)} fusion(bf16[2048,2048]{1,0:T(8,128)(2,1)} %get-tuple-element.294, f32[2048,512]{1,0:T(8,128)} %get-tuple-element.291, f32[]{:T(128)S(6)} %div.115), kind=kOutput, calls=%fused_computation.144 | convolution fusion | flops 4298113024 | bytes 14680068 | tf_op jit(solution)/shard_map/tf,td->fd/dot_general | solution.py:202
  453.6 34.1 %all-gather.12.cloned.1.call-done = bf16[8192,512]{1,0:T(8,128)(2,1)} async-done(((bf16[2048,512]{1,0:T(8,128)(2,1)}), bf16[8192,512]{1,0:T(8,128)(2,1)}) %all-gather.12.cloned.1.call-update) | async-done | bytes 8388624 | tf_op jit(solution)/shard_map/all_gather | solution.py:27
  487.8 7.1 convolution_convert_fusion.1
  494.9 8.6 reshape.233
  503.5 10.6 %copy.72 = bf16[8,2,512,2,64]{2,4,3,1,0:T(8,128)(2,1)} copy(bf16[8,2,512,2,64]{4,3,2,1,0:T(2,128)(2,1)} %reshape.233) | data formatting | bytes 4194304 | tf_op jit(solution)/shard_map/while | solution.py:233
  514.2 250.8 %while.29 = (s32[]{:T(128)}, f32[8,2,512,2,64]{2,4,3,1,0:T(8,128)}, f32[8,2,512,2,64]{2,1,0,4,3:T(2,128)}, f32[8,2,512,2,64]{2,4,3,1,0:T(8,128)}, bf16[8,2,512,2...) while((s32[]{:T(128)}, f32[8,2,512,2,64]{2,4,3,1,0:T(8,128)}, ...), condition=%wide.region_25.26_spmd.clone, body=%wide.region_23.25_spmd.sunk.clone | while | flops 687609856 | bytes 52209824 | solution.py:233
  525.2 8.4 fusion.202
  533.6 7.2 fusion.203
  556.9 8.1 fusion.202
  565.0 7.1 fusion.203
  588.3 8.0 fusion.202
  596.4 7.1 fusion.203
  619.6 8.0 fusion.202
  627.6 7.1 fusion.203
  650.8 8.1 fusion.202
  658.9 7.1 fusion.203
  682.1 8.1 fusion.202
  690.2 7.1 fusion.203
  713.4 8.0 fusion.202
  721.4 7.1 fusion.203
  744.7 8.0 fusion.202
  752.7 7.1 fusion.203
  764.9 7.4 copy.75
  772.4 6.6 stack_reshape.11
  778.9 6.8 stack_reshape.10
  785.7 7.3 copy.73
  793.0 6.6 stack_reshape.9
  807.4 7.6 fusion.104
  815.1 10.3 %bitcast_convert_fusion = bf16[8192,512]{1,0:T(8,128)(2,1)} fusion(bf16[3,512,128]{1,2,0:T(8,128)(2,1)S(1)} %copy-done.9, f32[3]{0:T(128)S(1)} %copy-done.23, f32[1,8192,128]{1,2,0:T(8,128)} %stack_reshape.11, f32[1,8192,128]{1,2,0:T(8,128)} %stack_reshape.10, f32[1,8192,128]{1,2,0:T(8,128)} %stack_reshape.9, f32[3]{0:T(128)S(1)} %copy-done.27), kind=kOutput, calls=%fused_computation.76 | convolution fusion | flops 3239575552 | bytes 21364760 | tf_op jit(solution)/shard_map/ith,idh->td/dot_general | solution.py:257
  827.3 6.5 all-reduce
  833.9 10.7 %all-reduce.2 = (f32[512]{0:T(512)S(1)}, f32[512]{0:T(512)S(1)}, f32[512]{0:T(512)S(1)}, f32[512]{0:T(512)S(1)}, f32[512]{0:T(512)S(1)}, /*index=5*/f32[512]{0:T(512)S(1)}) all-reduce(f32[512]{0:T(512)S(1)} %get-tuple-element.292, f32[512]{0:T(512)S(1)} %get-tuple-element.220, ...), channel_id=1, replica_groups=mesh['dp'=8,'tensor'=4] {'tensor'}, use_global_device_ids=true, to_apply=%region_33.34 | all-reduce | flops 3072 | bytes 24576 | tf_op jit(solution)/shard_map/psum | solution.py:278
  844.6 37.4 %all-reduce.1 = (f32[512]{0:T(512)}, f32[512]{0:T(512)}, f32[512]{0:T(512)}, f32[512]{0:T(512)}, f32[512]{0:T(512)}, /*index=5*/f32[512]{0:T(512)}) all-reduce(f32[512]{0:T(512)S(1)} %get-tuple-element.274, f32[512]{0:T(512)S(1)} %get-tuple-element.275, f32[512]{0:T(512)S(1)} %get-tuple-element.276, ...), channel_id=1, replica_groups=mesh['dp'=8,'tensor'=4] {'dp'}, use_global_device_ids=true, to_apply=%region_34.35 | all-reduce | flops 3072 | bytes 24576 | tf_op jit(solution)/shard_map/psum | solution.py:278
  888.8 18.1 %all-reduce.4 = (bf16[2,128]{1,0:T(2,128)(2,1)}, bf16[512]{0:T(512)(128)(2,1)S(1)}) all-reduce(bf16[2,128]{1,0:T(2,128)(2,1)S(1)} %pad_maximum_fusion, bf16[512]{0:T(512)(128)(2,1)S(1)} %dynamic-slice.1), channel_id=1, replica_groups=mesh['dp'=8,'tensor'=4] {'dp'}, use_global_device_ids=true, to_apply=%region_30.31 | all-reduce | flops 768 | bytes 3072 | tf_op jit(solution)/shard_map/psum | solution.py:263
  920.1 59.6 %reduce-scatter.7.cloned.1.call-done = bf16[2048,512]{1,0:T(8,128)(2,1)} async-done(((bf16[8192,512]{1,0:T(8,128)(2,1)}), bf16[2048,512]{1,0:T(8,128)(2,1)}) %reduce-scatter.7.cloned.1.call-update) | async-done | bytes 2097168 | tf_op jit(solution)/shard_map/reduce_scatter | solution.py:31
  979.7 6.6 fusion.92
  (323 shorter events, 294.8 us)
Async XLA Ops:
  7.2 50.3 %copy-start.19 = (bf16[3,512,128]{2,1,0:T(8,128)(2,1)S(1)}, bf16[3,512,128]{2,1,0:T(8,128)(2,1)}, u32[]{:S(2)}) copy-start(bf16[3,512,128]{2,1,0:T(8,128)(2,1)} %param.23) | copy-start | bytes 1179652
  7.2 50.5 %copy-start.17 = (bf16[128,512]{1,0:T(8,128)(2,1)S(1)}, bf16[128,512]{1,0:T(8,128)(2,1)}, u32[]{:S(2)}) copy-start(bf16[128,512]{1,0:T(8,128)(2,1)} %param.25) | copy-start | bytes 393220
  7.2 108.7 %all-gather.6.cloned.1.call-start = ((), (), s32[]{:S(2)}) async-start(), calls=%async_computation.4 | async-start | bytes 10485760 | tf_op jit(solution)/shard_map/all_gather | solution.py:27
  9.8 48.7 %copy-start.10 = (bf16[512,512]{1,0:T(8,128)(2,1)S(1)}, bf16[512,512]{1,0:T(8,128)(2,1)}, u32[]{:S(2)}) copy-start(bf16[512,512]{1,0:T(8,128)(2,1)} %param.29) | copy-start | bytes 1572868
  9.8 48.7 %copy-start.12 = (bf16[512,512]{1,0:T(8,128)(2,1)S(1)}, bf16[512,512]{1,0:T(8,128)(2,1)}, u32[]{:S(2)}) copy-start(bf16[512,512]{1,0:T(8,128)(2,1)} %param.31) | copy-start | bytes 1572868
  52.6 13.9 %copy-start.38 = (bf16[2,128]{1,0:T(2,128)(2,1)S(1)}, bf16[2,128]{1,0:T(2,128)(2,1)}, u32[]{:S(2)}) copy-start(bf16[2,128]{1,0:T(2,128)(2,1)} %param.24) | copy-start | bytes 1540
  52.6 14.0 %copy-start.21 = (s32[16,512]{1,0:T(8,128)S(1)}, s32[16,512]{1,0:T(8,128)}, u32[]{:S(2)}) copy-start(s32[16,512]{1,0:T(8,128)} %param.21) | copy-start | bytes 98308
  52.6 14.0 %copy-start.37 = (s32[16]{0:T(128)S(1)}, s32[16]{0:T(128)}, u32[]{:S(2)}) copy-start(s32[16]{0:T(128)} %param.22) | copy-start | bytes 196
  57.4 242.3 %reduce-scatter.5.cloned.1.call-start = ((), (), s32[]{:S(2)}) async-start(), calls=%async_computation.5 | async-start | bytes 10485760 | tf_op jit(solution)/shard_map/reduce_scatter | solution.py:31
  57.7 64.4 %copy-start.8 = (bf16[3,512,128]{1,2,0:T(8,128)(2,1)}, bf16[3,512,128]{1,2,0:T(8,128)(2,1)S(1)}, u32[]{:S(2)}) copy-start(bf16[3,512,128]{1,2,0:T(8,128)(2,1)S(1)} %copy.65) | copy-start | bytes 1179652
  69.1 53.0 %copy-start.22 = (f32[3]{0:T(128)}, f32[3]{0:T(128)S(1)}, u32[]{:S(2)}) copy-start(f32[3]{0:T(128)S(1)} %get-tuple-element.301) | copy-start | bytes 40
  69.1 53.0 %copy-start.26 = (f32[3]{0:T(128)}, f32[3]{0:T(128)S(1)}, u32[]{:S(2)}) copy-start(f32[3]{0:T(128)S(1)} %get-tuple-element.302) | copy-start | bytes 40
  142.2 4.2 copy-start.5
  146.4 3.6 copy-start.6
  213.7 8.4 copy-start.20
  213.7 8.4 copy-start.29
  222.1 5.7 copy-start.2
  227.8 4.2 copy-start.30
  227.8 4.3 copy-start.31
  227.8 9.5 copy-start.32
  227.8 9.5 copy-start.33
  227.8 9.5 copy-start.34
  227.8 9.5 copy-start.35
  227.9 9.5 copy-start.36
  227.9 71.9 %copy-start = (bf16[2048,512]{1,0:T(8,128)(2,1)S(1)}, bf16[2048,512]{1,0:T(8,128)(2,1)}, u32[]{:S(2)}) copy-start(bf16[2048,512]{1,0:T(8,128)(2,1)} %param.20) | copy-start | bytes 6291460
  227.9 96.7 %all-gather.8.cloned.1.call-start = ((), (), s32[]{:S(2)}) async-start(), calls=%async_computation.6 | async-start | bytes 2621440 | tf_op jit(solution)/shard_map/all_gather | solution.py:182
  230.0 140.6 %all-gather.10.cloned.1.call-start = ((), (), s32[]{:S(2)}) async-start(), calls=%async_computation.7 | async-start | bytes 2621440 | tf_op jit(solution)/shard_map/all_gather | solution.py:184
  232.0 255.8 %all-gather.12.cloned.1.call-start = ((), (), s32[]{:S(2)}) async-start(), calls=%async_computation.8 | async-start | bytes 10485760 | tf_op jit(solution)/shard_map/all_gather | solution.py:27
  299.8 2.6 copy-start.3
  379.6 1.6 copy-start.7
  411.4 11.7 %copy-start.4 = (bf16[2048,512]{1,0:T(8,128)(2,1)S(1)}, bf16[2048,512]{1,0:T(8,128)(2,1)}, u32[]{:S(2)}) copy-start(bf16[2048,512]{1,0:T(8,128)(2,1)} %reduce-scatter.5.cloned.1.call-done) | copy-start | bytes 6291460
  425.4 2.0 copy-start.1
  429.3 385.7 %reduce-scatter.9.cloned.1.call-start = ((), (), s32[]{:S(2)}) async-start(), calls=%async_computation.10 | async-start | bytes 2621440 | tf_op jit(solution)/shard_map/reduce_scatter | solution.py:210
  443.0 372.1 %reduce-scatter.11.cloned.1.call-start = ((), (), s32[]{:S(2)}) async-start(), calls=%async_computation.11 | async-start | bytes 2621440 | tf_op jit(solution)/shard_map/reduce_scatter | solution.py:216
  443.1 44.7 %copy-start.18 = (bf16[128,512]{1,0:T(8,128)(2,1)S(1)}, bf16[128,512]{1,0:T(8,128)(2,1)}, u32[]{:S(2)}) copy-start(bf16[128,512]{1,0:T(8,128)(2,1)} %param.25) | copy-start | bytes 393220
  453.6 455.1 %all-reduce.8.cloned.1.call-start = ((), (), s32[]{:S(2)}) async-start(), calls=%async_computation.12 | async-start | bytes 3145728 | tf_op jit(solution)/shard_map/psum | solution.py:262
  799.7 6.1 copy-start.14
  799.7 6.5 copy-start.15
  799.7 7.7 copy-start.16
  799.7 7.7 copy-start.27
  807.4 7.7 copy-start.9
  807.4 7.7 copy-start.23
  815.1 164.7 %reduce-scatter.7.cloned.1.call-start = ((), (), s32[]{:S(2)}) async-start(), calls=%async_computation.9 | async-start | bytes 10485760 | tf_op jit(solution)/shard_map/reduce_scatter | solution.py:31
  825.4 8.5 copy-start.24
  825.4 8.5 copy-start.25
  825.4 8.5 copy-start.28
  884.6 30.4 %copy-start.11 = (bf16[512,512]{1,0:T(8,128)(2,1)S(1)}, bf16[512,512]{1,0:T(8,128)(2,1)}, u32[]{:S(2)}) copy-start(bf16[512,512]{1,0:T(8,128)(2,1)} %param.29) | copy-start | bytes 1572868
  884.6 32.9 %copy-start.13 = (bf16[512,512]{1,0:T(8,128)(2,1)S(1)}, bf16[512,512]{1,0:T(8,128)(2,1)}, u32[]{:S(2)}) copy-start(bf16[512,512]{1,0:T(8,128)(2,1)} %param.31) | copy-start | bytes 1572868
  (1 other events, 0.7 us)
Sparse Core Ops, SparseCore 0:
  57.6 58.2 all-gather.5
  228.0 71.7 reduce-scatter.4
  302.0 22.5 all-gather.7
  326.7 22.5 all-gather.9
  429.4 58.2 all-gather.11
  490.3 31.4 reduce-scatter.8
  524.3 31.4 reduce-scatter.10
  815.2 90.3 all-reduce.7
  908.4 71.3 reduce-scatter.6
